TPU v7x, 256 devices: a whole 4x4x8 slice. The times are simulated.
256 devices in a mesh: slab: 64 (over y, x_lo, z), view: 4 (over x_hi, core).
Axes of the slice: x: 4 (x_hi: 2, x_lo: 2; x = x_hi * 2 + x_lo), y: 4, z: 8, core: 2. Of those that a mesh axis runs over, the one named last changes fastest.
Arguments:
- primal: float32 [5, 256, 32, 128], P(None, 'slab', 'view'), may hold values from -6 to 6
- dual: bfloat16 [64, 256, 128], P('view', 'slab'), may hold values from -6 to 6
- footprints: bfloat16 [8, 128, 128], replicated, may hold values from -0.046875 to 0.046875
- tile_index: int32 [64, 8192, 2], P(None, 'slab'), may hold values from 0 to 3
- footprint_offset: int32 [64, 8192, 2], P(None, 'slab'), may hold values from 0 to 7
- w_first: bfloat16 [3, 3, 3, 32, 6], replicated, may hold values from -0.21875 to 0.21875
- w_middle: bfloat16 [3, 3, 3, 32, 32], replicated, may hold values from -0.21875 to 0.21875
- w_last: bfloat16 [3, 3, 3, 5, 32], replicated, may hold values from -0.5 to 0.5
- cotangent: float32 [5, 256, 32, 128], P(None, 'slab', 'view'), may hold values from -6 to 6
Outputs:
- d_primal: float32 [5, 256, 32, 128], P(None, 'slab', 'view')
- d_dual: float32 [64, 256, 128], P('view', 'slab')
- d_first: float32 [3, 3, 3, 32, 6], replicated
- d_middle: float32 [3, 3, 3, 32, 32], replicated
- d_last: float32 [3, 3, 3, 5, 32], replicated
All inputs are finite; a program needn't handle non-finite values.
Results may differ from a plain program's by a relative error of at most 0.0067.
Values may be sent and summed in bfloat16 or wider, within the bound.
No kernel may reach another device: no remote copies, remote signals or barrier semaphores. Data moves between devices by JAX's collectives and lax.ppermute only.
A program may use at most 64 MiB of HBM per device.

v0:
```python
import math
import jax
import jax.numpy as jnp
from jax import lax
from jax.sharding import PartitionSpec as P


def with_halo(cells, sides, width):
    for axis, dim in sides:
        count = lax.axis_size(axis)
        ends = count - 1
        head = lax.slice_in_dim(cells, 0, width, axis=dim)
        tail = lax.slice_in_dim(cells, cells.shape[dim] - width, cells.shape[dim], axis=dim)
        cells = jnp.concatenate(
            [
                lax.ppermute(tail, axis, [(i, (i + 1) % count) for i in range(ends)]),
                cells,
                lax.ppermute(head, axis, [((i + 1) % count, i) for i in range(ends)]),
            ],
            axis=dim,
        )
    return cells


def silu_slope(value):
    sig = jax.nn.sigmoid(value)
    return sig * (1.0 + value * (1.0 - sig))


def flipped(kernel):
    return kernel[::-1, ::-1, ::-1].transpose(0, 1, 2, 4, 3)


def sideways(padded):
    blank = jnp.zeros(padded.shape[:-1] + (1,), padded.dtype)
    left = jnp.concatenate([blank, padded[..., :-1]], axis=-1)
    right = jnp.concatenate([padded[..., 1:], blank], axis=-1)
    return (left, padded, right)


def rims(field):
    return with_halo(field, (("slab", 1), ("view", 2)), 1)


def convolve(parts, kernel, depth, rows):
    total = None
    for za in range(3):
        for yb in range(3):
            for xc in range(3):
                term = jnp.einsum(
                    "oc,czyx->ozyx",
                    kernel[za, yb, xc],
                    parts[xc][:, za : za + depth, yb : yb + rows, :],
                    preferred_element_type=jnp.float32,
                )
                total = term if total is None else total + term
    return total


def kernel_grad(dout, parts, depth, rows):
    terms = []
    for za in range(3):
        for yb in range(3):
            for xc in range(3):
                terms.append(
                    jnp.einsum(
                        "ozyx,czyx->oc",
                        dout,
                        parts[xc][:, za : za + depth, yb : yb + rows, :],
                        preferred_element_type=jnp.float32,
                    )
                )
    return jnp.stack(terms).reshape(3, 3, 3, dout.shape[0], parts[0].shape[0])


def shards(
    primal, dual, footprints, tile_index, footprint_offset, w_first, w_middle, w_last, cotangent
):
    channels, depth, rows_here, width = primal.shape
    views_here, det_tiles, bins = dual.shape
    all_views = tile_index.shape[0]
    taps = tile_index.shape[2]
    foot_count = footprints.shape[0]
    n_view = lax.axis_size("view")
    full_rows = rows_here * n_view
    x_tiles = width // bins
    view_at = lax.axis_index("view")
    forward_mat = footprints.transpose(1, 0, 2).reshape(bins, foot_count * bins)
    backward_mat = footprints.transpose(2, 0, 1).reshape(bins, foot_count * bins)
    tile_grid = tile_index.reshape(all_views, depth, full_rows, x_tiles, taps)
    foot_grid = footprint_offset.reshape(all_views, depth, full_rows, x_tiles, taps)
    stride = det_tiles * foot_count
    heights = jnp.dot(
        dual.reshape(-1, bins), forward_mat, preferred_element_type=jnp.float32
    ).reshape(-1, bins)
    own_tiles = lax.dynamic_slice_in_dim(tile_grid, view_at * views_here, views_here, 0)
    own_foot = lax.dynamic_slice_in_dim(foot_grid, view_at * views_here, views_here, 0)
    count = rows_here * lax.axis_size("view")

    def strip_add_view(view, total):
        picks = view * stride + own_tiles[view] * foot_count + own_foot[view]
        return total + jnp.take(heights, picks, axis=0).sum(axis=3)

    total = lax.fori_loop(
        0, views_here, strip_add_view, jnp.zeros((depth, count, x_tiles, bins), jnp.float32)
    )
    strips = lax.psum_scatter(
        total.reshape(depth, count, width).transpose(1, 0, 2),
        "view",
        scatter_dimension=0,
        tiled=True,
    )
    back = strips.transpose(1, 0, 2)
    x_zero = jnp.concatenate([primal, back[None]], axis=0).astype(jnp.bfloat16)
    g_low = cotangent.astype(jnp.bfloat16)
    x_parts = sideways(with_halo(x_zero, (("slab", 1), ("view", 2)), 1))
    g_parts = sideways(with_halo(g_low, (("slab", 1), ("view", 2)), 1))
    a_one = convolve(x_parts, w_first, depth, rows_here)
    z_one = jax.nn.silu(a_one).astype(jnp.bfloat16)
    z_one_parts = sideways(rims(z_one))
    a_two = convolve(z_one_parts, w_middle, depth, rows_here)
    z_two = jax.nn.silu(a_two).astype(jnp.bfloat16)
    z_two_parts = sideways(rims(z_two))
    dz_two = convolve(g_parts, flipped(w_last), depth, rows_here)
    d_last = kernel_grad(g_low, z_two_parts, depth, rows_here)
    da_two = (dz_two * silu_slope(a_two)).astype(jnp.bfloat16)
    dz_one = convolve(sideways(rims(da_two)), flipped(w_middle), depth, rows_here)
    d_middle = kernel_grad(da_two, z_one_parts, depth, rows_here)
    da_one = (dz_one * silu_slope(a_one)).astype(jnp.bfloat16)
    dx_zero = convolve(sideways(rims(da_one)), flipped(w_first), depth, rows_here)
    d_first = kernel_grad(da_one, x_parts, depth, rows_here)
    d_primal = cotangent + dx_zero[:channels]
    strip_grad = dx_zero[channels].astype(jnp.bfloat16)
    start_grad = jnp.zeros((views_here * det_tiles, bins), jnp.float32)
    piece = lax.all_gather(strip_grad, "view", axis=1, tiled=True)
    count = piece.shape[1]
    proj = jnp.dot(
        piece.reshape(-1, bins), backward_mat, preferred_element_type=jnp.float32
    ).reshape(-1, bins)
    tile_ids = jnp.arange(depth * count * x_tiles, dtype=jnp.int32).reshape(
        depth, count, x_tiles, 1
    )

    def fold_add_view(view, acc):
        source = tile_ids * foot_count + own_foot[view]
        target = view * det_tiles + own_tiles[view]
        return acc + jax.ops.segment_sum(
            jnp.take(proj, source.reshape(-1), axis=0),
            target.reshape(-1),
            num_segments=views_here * det_tiles,
        )

    d_dual = lax.fori_loop(0, views_here, fold_add_view, start_grad).reshape(
        views_here, det_tiles, bins
    )
    summed = lax.psum((d_first, d_middle, d_last), ("slab", "view"))
    scale = 1.0 / math.sqrt(depth * lax.axis_size("slab") * full_rows * width)
    return (d_primal, d_dual, summed[0] * scale, summed[1] * scale, summed[2] * scale)


def solution(mesh):
    placed = (
        P(None, "slab", "view", None),
        P("view", "slab", None),
        P(),
        P(None, "slab", None),
        P(None, "slab", None),
        P(),
        P(),
        P(),
        P(None, "slab", "view", None),
    )
    return jax.shard_map(
        shards,
        mesh=mesh,
        in_specs=placed,
        out_specs=(P(None, "slab", "view", None), P("view", "slab", None), P(), P(), P()),
        check_vma=False,
    )
```

profile of v0, /device:TPU:1, one launch (start us, length us, event | category | flops | bytes accessed | tf_op | source)
XLA Modules:
  0.0 618.3 jit_solution(12563308730298618970)
XLA Ops:
  7.3 3.5 copy.388
  10.8 2.7 copy.389
  15.7 21.8 %while.30 = (s32[]{:T(128)}, f32[4,32,1,128]{3,2,1,0:T(1,128)S(1)}, s32[16,4,32,1,2]{4,2,1,3,0:T(8,128)S(1)}, s32[16,4,32,1,2]{4,2,1,3,0:T(8,128)S(1)}, f32[512,...) while((s32[]{:T(128)}, f32[4,32,1,128]{3,2,1,0:T(1,128)S(1)}, ...), condition=%wide.region_2.3_spmd.clone, body=%wide.region_0.2_spmd.clone.sunk | while | flops 86788 | bytes 669307 | solution.py:104
  38.3 4.4 collective-permute-start
  44.8 2.4 collective-permute-done.1
  47.3 6.5 %collective-permute-start.2 = (bf16[5,6,1,128]{3,2,1,0:T(2,128)(2,1)S(1)}, bf16[5,6,1,128]{3,2,1,0:T(2,128)(2,1)S(1)}, u32[]{:S(2)}, u32[]{:S(2)}) collective-permute-start(bf16[5,6,1,128]{3,2,1,0:T(2,128)(2,1)S(1)} %get-tuple-element.443), channel_id=1, source_target_pairs={{0,1},{1,2},{2,3},{4,5},{5,6},{6,7},{8,9},{9,10},{10,11},{12,13},{... | collective-permute-start | bytes 23048 | tf_op jit(solution)/shard_map/ppermute | solution.py:16
  53.7 1.9 collective-permute-start.3
  55.7 4.6 collective-permute-done.3
  68.7 4.5 reduce-scatter.2.cloned.1.call-done
  73.9 3.2 collective-permute-start.4
  79.4 2.1 collective-permute-done.5
  81.5 4.7 collective-permute-start.6
  86.3 1.9 collective-permute-start.7
  88.3 4.6 collective-permute-done.7
  106.4 3.2 collective-permute-start.8
  112.3 2.8 collective-permute-done.9
  115.2 3.1 collective-permute-start.10
  120.3 4.9 collective-permute-done.11
  158.0 4.8 collective-permute-start.20
  164.1 4.3 collective-permute-start.12
  169.7 240.3 %all-reduce.15.cloned.1.call-done = f32[3,3,3,32,32]{4,3,2,1,0:T(8,128)} async-done(((f32[3,3,3,32,32]{4,3,2,1,0:T(8,128)}), f32[3,3,3,32,32]{4,3,2,1,0:T(8,128)}) %all-reduce.15.cloned.1.call-update) | async-done | bytes 110608 | tf_op jit(solution)/shard_map/psum | solution.py:156
  411.8 5.5 collective-permute-start.22
  417.3 1.9 collective-permute-start.23
  419.3 5.1 collective-permute-start.14
  424.5 2.1 collective-permute-start.15
  426.6 4.8 collective-permute-done.15
  453.8 80.9 %all-reduce.12 = (f32[3,3,3,32,6]{3,4,2,1,0:T(8,128)S(1)}, f32[3,3,3,5,32]{4,2,3,1,0:T(4,128)S(1)}) all-reduce(f32[3,3,3,32,6]{3,4,2,1,0:T(8,128)} %bitcast.1969, f32[3,3,3,5,32]{4,2,3,1,0:T(4,128)S(1)} %copy.582), channel_id=1, replica_groups=mesh['slab'=64,'view'=4] {'slab','view'}, use_global_device_ids=true, to_apply=%region_7.8 | all-reduce | flops 9504 | bytes 76032 | tf_op jit(solution)/shard_map/psum | solution.py:156
  535.4 3.8 collective-permute-start.18
  539.2 2.1 collective-permute-start.19
  542.0 4.1 collective-permute-done.19
  551.5 5.6 all-gather
  557.4 53.1 %while.29 = (s32[]{:T(128)}, f32[64,128]{1,0:T(8,128)S(1)}, s32[16,4,32,1,2]{4,2,1,3,0:T(8,128)S(1)}, s32[16,4,32,1,2]{4,2,1,3,0:T(8,128)S(1)}, f32[1024,128]{1,...) while((s32[]{:T(128)}, f32[64,128]{1,0:T(8,128)S(1)}, ...), condition=%wide.region_6.7_spmd.clone.clone, body=%wide.region_4.6_spmd.clone.clone.sunk | while | flops 70019 | bytes 588653 | solution.py:153
  558.3 2.4 scatter_custom_fusion.6
  561.6 2.4 scatter_custom_fusion.6
  565.0 2.4 scatter_custom_fusion.6
  568.3 2.4 scatter_custom_fusion.6
  571.6 2.4 scatter_custom_fusion.6
  574.9 2.4 scatter_custom_fusion.6
  578.2 2.4 scatter_custom_fusion.6
  581.5 2.4 scatter_custom_fusion.6
  584.9 2.4 scatter_custom_fusion.6
  588.2 2.4 scatter_custom_fusion.6
  591.5 2.4 scatter_custom_fusion.6
  594.8 2.4 scatter_custom_fusion.6
  598.1 2.4 scatter_custom_fusion.6
  601.4 2.4 scatter_custom_fusion.6
  604.8 2.4 scatter_custom_fusion.6
  608.1 2.4 scatter_custom_fusion.6
  (727 shorter events, 134.8 us)
Async XLA Ops:
  7.2 66.0 %reduce-scatter.2.cloned.1.call-start = ((), (), s32[]{:S(2)}) async-start(), calls=%async_computation.1 | async-start | bytes 81920 | tf_op jit(solution)/shard_map/reduce_scatter | solution.py:107
  15.7 22.5 %copy-start.6 = (f32[5,4,8,128]{3,2,1,0:T(8,128)S(1)}, f32[5,4,8,128]{3,2,1,0:T(8,128)}, u32[]{:S(2)}) copy-start(f32[5,4,8,128]{3,2,1,0:T(8,128)} %param.21) | copy-start | bytes 245764
  15.7 28.2 %copy-start.58 = (bf16[3,3,3,5,32]{4,2,3,1,0:T(4,128)(2,1)S(1)}, bf16[3,3,3,5,32]{4,2,3,1,0:T(4,128)(2,1)}, u32[]{:S(2)}) copy-start(bf16[3,3,3,5,32]{4,2,3,1,0:T(4,128)(2,1)} %param.20) | copy-start | bytes 25924
  15.7 28.3 %copy-start.5 = (bf16[3,3,3,32,32]{4,3,2,1,0:T(8,128)(2,1)S(1)}, bf16[3,3,3,32,32]{4,3,2,1,0:T(8,128)(2,1)}, u32[]{:S(2)}) copy-start(bf16[3,3,3,32,32]{4,3,2,1,0:T(8,128)(2,1)} %param.19) | copy-start | bytes 165892
  15.7 28.5 %copy-start.49 = (bf16[3,3,3,32,6]{3,4,2,1,0:T(8,128)(2,1)S(1)}, bf16[3,3,3,32,6]{3,4,2,1,0:T(8,128)(2,1)}, u32[]{:S(2)}) copy-start(bf16[3,3,3,32,6]{3,4,2,1,0:T(8,128)(2,1)} %param.18) | copy-start | bytes 31108
  15.7 29.1 %copy-start.54 = (f32[5,4,8,128]{3,2,1,0:T(8,128)S(1)}, f32[5,4,8,128]{3,2,1,0:T(8,128)}, u32[]{:S(2)}) copy-start(f32[5,4,8,128]{3,2,1,0:T(8,128)} %param.13) | copy-start | bytes 245764
  38.2 371.8 %all-reduce.15.cloned.1.call-start = ((), (), s32[]{:S(2)}) async-start(), calls=%async_computation.2 | async-start | bytes 884736 | tf_op jit(solution)/shard_map/psum | solution.py:156
  38.3 6.6 %collective-permute-start = (bf16[5,1,8,128]{3,2,1,0:T(8,128)(2,1)S(1)}, bf16[5,1,8,128]{3,2,1,0:T(8,128)(2,1)S(1)}, u32[]{:S(2)}, u32[]{:S(2)}) collective-permute-start(bf16[5,1,8,128]{3,2,1,0:T(8,128)(2,1)S(1)} %get-tuple-element.452), channel_id=1, source_target_pairs={{0,4},{4,8},{8,12},{12,16},{16,20},{20,24},{24,28},{28,32},{32,36}... | collective-permute-start | bytes 30728 | tf_op jit(solution)/shard_map/ppermute | solution.py:16
  42.6 4.6 collective-permute-start.1
  44.0 23.4 %copy-start.51 = (bf16[3,3,3,32,5]{3,4,2,1,0:T(8,128)(2,1)}, bf16[3,3,3,32,5]{3,4,2,1,0:T(8,128)(2,1)S(1)}, u32[]{:S(2)}) copy-start(bf16[3,3,3,32,5]{3,4,2,1,0:T(8,128)(2,1)S(1)} %reverse_bitcast_fusion.2) | copy-start | bytes 25924
  47.3 8.4 %collective-permute-start.2 = (bf16[5,6,1,128]{3,2,1,0:T(2,128)(2,1)S(1)}, bf16[5,6,1,128]{3,2,1,0:T(2,128)(2,1)S(1)}, u32[]{:S(2)}, u32[]{:S(2)}) collective-permute-start(bf16[5,6,1,128]{3,2,1,0:T(2,128)(2,1)S(1)} %get-tuple-element.443), channel_id=1, source_target_pairs={{0,1},{1,2},{2,3},{4,5},{5,6},{6,7},{8,9},{9,10},{10,11},{12,13},{... | collective-permute-start | bytes 23048 | tf_op jit(solution)/shard_map/ppermute | solution.py:16
  53.7 6.6 %collective-permute-start.3 = (bf16[5,6,1,128]{3,2,1,0:T(2,128)(2,1)S(1)}, bf16[5,6,1,128]{3,2,1,0:T(2,128)(2,1)S(1)}, u32[]{:S(2)}, u32[]{:S(2)}) collective-permute-start(bf16[5,6,1,128]{3,2,1,0:T(2,128)(2,1)S(1)} %get-tuple-element.444), channel_id=1, source_target_pairs={{1,0},{2,1},{3,2},{5,4},{6,5},{7,6},{9,8},{10,9},{11,10},{13,12},{... | collective-permute-start | bytes 23048 | tf_op jit(solution)/shard_map/ppermute | solution.py:18
  73.9 5.5 collective-permute-start.4
  77.1 4.4 collective-permute-start.5
  78.4 21.2 %copy-start.50 = (bf16[3,3,3,32,6]{3,4,2,1,0:T(8,128)(2,1)S(1)}, bf16[3,3,3,32,6]{3,4,2,1,0:T(8,128)(2,1)}, u32[]{:S(2)}) copy-start(bf16[3,3,3,32,6]{3,4,2,1,0:T(8,128)(2,1)} %param.18) | copy-start | bytes 31108
  81.5 6.7 %collective-permute-start.6 = (bf16[6,6,1,128]{3,2,1,0:T(2,128)(2,1)S(1)}, bf16[6,6,1,128]{3,2,1,0:T(2,128)(2,1)S(1)}, u32[]{:S(2)}, u32[]{:S(2)}) collective-permute-start(bf16[6,6,1,128]{3,2,1,0:T(2,128)(2,1)S(1)} %get-tuple-element.440), channel_id=1, source_target_pairs={{0,1},{1,2},{2,3},{4,5},{5,6},{6,7},{8,9},{9,10},{10,11},{12,13},{... | collective-permute-start | bytes 27656 | tf_op jit(solution)/shard_map/ppermute | solution.py:16
  86.3 6.6 %collective-permute-start.7 = (bf16[6,6,1,128]{3,2,1,0:T(2,128)(2,1)S(1)}, bf16[6,6,1,128]{3,2,1,0:T(2,128)(2,1)S(1)}, u32[]{:S(2)}, u32[]{:S(2)}) collective-permute-start(bf16[6,6,1,128]{3,2,1,0:T(2,128)(2,1)S(1)} %get-tuple-element.439), channel_id=1, source_target_pairs={{1,0},{2,1},{3,2},{5,4},{6,5},{7,6},{9,8},{10,9},{11,10},{13,12},{... | collective-permute-start | bytes 27656 | tf_op jit(solution)/shard_map/ppermute | solution.py:18
  88.2 12.0 %copy-start.17 = (bf16[6,4,8,128]{3,2,1,0:T(8,128)(2,1)}, bf16[6,4,8,128]{3,2,1,0:T(8,128)(2,1)S(1)}, u32[]{:S(2)}) copy-start(bf16[6,4,8,128]{3,2,1,0:T(8,128)(2,1)S(1)} %get-tuple-element.446) | copy-start | bytes 147460
  93.3 7.2 %copy-start.25 = (bf16[6,4,8,128]{3,2,1,0:T(8,128)(2,1)}, bf16[6,4,8,128]{3,2,1,0:T(8,128)(2,1)S(1)}, u32[]{:S(2)}) copy-start(bf16[6,4,8,128]{3,2,1,0:T(8,128)(2,1)S(1)} %get-tuple-element.399) | copy-start | bytes 147460
  93.3 8.0 %copy-start.21 = (bf16[6,4,8,128]{3,2,1,0:T(8,128)(2,1)}, bf16[6,4,8,128]{3,2,1,0:T(8,128)(2,1)S(1)}, u32[]{:S(2)}) copy-start(bf16[6,4,8,128]{3,2,1,0:T(8,128)(2,1)S(1)} %get-tuple-element.400) | copy-start | bytes 147460
  93.3 8.9 %copy-start.15 = (bf16[6,4,8,128]{3,2,1,0:T(8,128)(2,1)}, bf16[6,4,8,128]{3,2,1,0:T(8,128)(2,1)S(1)}, u32[]{:S(2)}) copy-start(bf16[6,4,8,128]{3,2,1,0:T(8,128)(2,1)S(1)} %get-tuple-element.401) | copy-start | bytes 147460
  93.3 9.7 %copy-start.7 = (bf16[6,4,8,128]{3,2,1,0:T(8,128)(2,1)}, bf16[6,4,8,128]{3,2,1,0:T(8,128)(2,1)S(1)}, u32[]{:S(2)}) copy-start(bf16[6,4,8,128]{3,2,1,0:T(8,128)(2,1)S(1)} %get-tuple-element.402) | copy-start | bytes 147460
  94.5 7.2 %copy-start.31 = (bf16[6,4,8,128]{3,2,1,0:T(8,128)(2,1)}, bf16[6,4,8,128]{3,2,1,0:T(8,128)(2,1)S(1)}, u32[]{:S(2)}) copy-start(bf16[6,4,8,128]{3,2,1,0:T(8,128)(2,1)S(1)} %get-tuple-element.406) | copy-start | bytes 147460
  94.6 7.3 %copy-start.35 = (bf16[6,4,8,128]{3,2,1,0:T(8,128)(2,1)}, bf16[6,4,8,128]{3,2,1,0:T(8,128)(2,1)S(1)}, u32[]{:S(2)}) copy-start(bf16[6,4,8,128]{3,2,1,0:T(8,128)(2,1)S(1)} %get-tuple-element.388) | copy-start | bytes 147460
  94.7 8.1 %copy-start.27 = (bf16[6,4,8,128]{3,2,1,0:T(8,128)(2,1)}, bf16[6,4,8,128]{3,2,1,0:T(8,128)(2,1)S(1)}, u32[]{:S(2)}) copy-start(bf16[6,4,8,128]{3,2,1,0:T(8,128)(2,1)S(1)} %get-tuple-element.389) | copy-start | bytes 147460
  94.7 9.0 %copy-start.19 = (bf16[6,4,8,128]{3,2,1,0:T(8,128)(2,1)}, bf16[6,4,8,128]{3,2,1,0:T(8,128)(2,1)S(1)}, u32[]{:S(2)}) copy-start(bf16[6,4,8,128]{3,2,1,0:T(8,128)(2,1)S(1)} %get-tuple-element.391) | copy-start | bytes 147460
  94.7 9.8 %copy-start.9 = (bf16[6,4,8,128]{3,2,1,0:T(8,128)(2,1)}, bf16[6,4,8,128]{3,2,1,0:T(8,128)(2,1)S(1)}, u32[]{:S(2)}) copy-start(bf16[6,4,8,128]{3,2,1,0:T(8,128)(2,1)S(1)} %get-tuple-element.392) | copy-start | bytes 147460
  94.7 10.6 %copy-start.56 = (bf16[6,4,8,128]{3,2,1,0:T(8,128)(2,1)}, bf16[6,4,8,128]{3,2,1,0:T(8,128)(2,1)S(1)}, u32[]{:S(2)}) copy-start(bf16[6,4,8,128]{3,2,1,0:T(8,128)(2,1)S(1)} %get-tuple-element.385) | copy-start | bytes 147460
  95.7 7.6 %copy-start.33 = (bf16[6,4,8,128]{3,2,1,0:T(8,128)(2,1)}, bf16[6,4,8,128]{3,2,1,0:T(8,128)(2,1)S(1)}, u32[]{:S(2)}) copy-start(bf16[6,4,8,128]{3,2,1,0:T(8,128)(2,1)S(1)} %get-tuple-element.395) | copy-start | bytes 147460
  95.8 9.3 %copy-start.13 = (bf16[6,4,8,128]{3,2,1,0:T(8,128)(2,1)}, bf16[6,4,8,128]{3,2,1,0:T(8,128)(2,1)S(1)}, u32[]{:S(2)}) copy-start(bf16[6,4,8,128]{3,2,1,0:T(8,128)(2,1)S(1)} %get-tuple-element.394) | copy-start | bytes 147460
  106.4 5.9 collective-permute-start.8
  109.6 5.6 collective-permute-start.9
  115.2 5.1 collective-permute-start.10
  118.3 6.9 %collective-permute-start.11 = (bf16[32,6,1,128]{3,0,2,1:T(8,128)(2,1)S(1)}, bf16[32,6,1,128]{3,0,2,1:T(8,128)(2,1)S(1)}, u32[]{:S(2)}, u32[]{:S(2)}) collective-permute-start(bf16[32,6,1,128]{3,0,2,1:T(8,128)(2,1)S(1)} %get-tuple-element.372), channel_id=1, source_target_pairs={{1,0},{2,1},{3,2},{5,4},{6,5},{7,6},{9,8},{10,9},{11,10},{13,12},{... | collective-permute-start | bytes 147464 | tf_op jit(solution)/shard_map/ppermute | solution.py:18
  158.0 253.8 %collective-permute-start.20 = (bf16[32,1,8,128]{3,0,2,1:T(8,128)(2,1)}, bf16[32,1,8,128]{3,0,2,1:T(8,128)(2,1)S(1)}, u32[]{:S(2)}, u32[]{:S(2)}) collective-permute-start(bf16[32,1,8,128]{3,0,2,1:T(8,128)(2,1)} %get-tuple-element.375), channel_id=1, source_target_pairs={{0,4},{4,8},{8,12},{12,16},{16,20},{20,24},{24,28},{28,32},{32,36}... | collective-permute-start | bytes 196616 | tf_op jit(solution)/shard_map/ppermute | solution.py:16
  162.8 249.0 %collective-permute-start.21 = (bf16[32,1,8,128]{3,0,2,1:T(8,128)(2,1)}, bf16[32,1,8,128]{3,0,2,1:T(8,128)(2,1)S(1)}, u32[]{:S(2)}, u32[]{:S(2)}) collective-permute-start(bf16[32,1,8,128]{3,0,2,1:T(8,128)(2,1)} %get-tuple-element.376), channel_id=1, source_target_pairs={{4,0},{8,4},{12,8},{16,12},{20,16},{24,20},{28,24},{32,28},{36,32}... | collective-permute-start | bytes 196616 | tf_op jit(solution)/shard_map/ppermute | solution.py:18
  164.1 255.2 %collective-permute-start.12 = (bf16[32,1,8,128]{3,0,2,1:T(8,128)(2,1)}, bf16[32,1,8,128]{3,0,2,1:T(8,128)(2,1)S(1)}, u32[]{:S(2)}, u32[]{:S(2)}) collective-permute-start(bf16[32,1,8,128]{3,0,2,1:T(8,128)(2,1)} %get-tuple-element.379), channel_id=1, source_target_pairs={{0,4},{4,8},{8,12},{12,16},{16,20},{20,24},{24,28},{28,32},{32,36}... | collective-permute-start | bytes 196616 | tf_op jit(solution)/shard_map/ppermute | solution.py:16
  168.4 250.9 %collective-permute-start.13 = (bf16[32,1,8,128]{3,0,2,1:T(8,128)(2,1)}, bf16[32,1,8,128]{3,0,2,1:T(8,128)(2,1)S(1)}, u32[]{:S(2)}, u32[]{:S(2)}) collective-permute-start(bf16[32,1,8,128]{3,0,2,1:T(8,128)(2,1)} %get-tuple-element.380), channel_id=1, source_target_pairs={{4,0},{8,4},{12,8},{16,12},{20,16},{24,20},{28,24},{32,28},{36,32}... | collective-permute-start | bytes 196616 | tf_op jit(solution)/shard_map/ppermute | solution.py:18
  411.8 27.3 %collective-permute-start.22 = (bf16[32,6,1,128]{3,0,2,1:T(8,128)(2,1)S(1)}, bf16[32,6,1,128]{3,0,2,1:T(8,128)(2,1)S(1)}, u32[]{:S(2)}, u32[]{:S(2)}) collective-permute-start(bf16[32,6,1,128]{3,0,2,1:T(8,128)(2,1)S(1)} %get-tuple-element.361), channel_id=1, source_target_pairs={{0,1},{1,2},{2,3},{4,5},{5,6},{6,7},{8,9},{9,10},{10,11},{12,13},{... | collective-permute-start | bytes 147464 | tf_op jit(solution)/shard_map/ppermute | solution.py:16
  417.3 21.8 %collective-permute-start.23 = (bf16[32,6,1,128]{3,0,2,1:T(8,128)(2,1)S(1)}, bf16[32,6,1,128]{3,0,2,1:T(8,128)(2,1)S(1)}, u32[]{:S(2)}, u32[]{:S(2)}) collective-permute-start(bf16[32,6,1,128]{3,0,2,1:T(8,128)(2,1)S(1)} %get-tuple-element.362), channel_id=1, source_target_pairs={{1,0},{2,1},{3,2},{5,4},{6,5},{7,6},{9,8},{10,9},{11,10},{13,12},{... | collective-permute-start | bytes 147464 | tf_op jit(solution)/shard_map/ppermute | solution.py:18
  419.3 7.3 %collective-permute-start.14 = (bf16[32,6,1,128]{3,0,2,1:T(8,128)(2,1)S(1)}, bf16[32,6,1,128]{3,0,2,1:T(8,128)(2,1)S(1)}, u32[]{:S(2)}, u32[]{:S(2)}) collective-permute-start(bf16[32,6,1,128]{3,0,2,1:T(8,128)(2,1)S(1)} %get-tuple-element.367), channel_id=1, source_target_pairs={{0,1},{1,2},{2,3},{4,5},{5,6},{6,7},{8,9},{9,10},{10,11},{12,13},{... | collective-permute-start | bytes 147464 | tf_op jit(solution)/shard_map/ppermute | solution.py:16
  424.5 6.9 %collective-permute-start.15 = (bf16[32,6,1,128]{3,0,2,1:T(8,128)(2,1)S(1)}, bf16[32,6,1,128]{3,0,2,1:T(8,128)(2,1)S(1)}, u32[]{:S(2)}, u32[]{:S(2)}) collective-permute-start(bf16[32,6,1,128]{3,0,2,1:T(8,128)(2,1)S(1)} %get-tuple-element.368), channel_id=1, source_target_pairs={{1,0},{2,1},{3,2},{5,4},{6,5},{7,6},{9,8},{10,9},{11,10},{13,12},{... | collective-permute-start | bytes 147464 | tf_op jit(solution)/shard_map/ppermute | solution.py:18
  450.9 84.4 %collective-permute-start.16 = (bf16[32,1,8,128]{3,0,2,1:T(8,128)(2,1)}, bf16[32,1,8,128]{3,0,2,1:T(8,128)(2,1)S(1)}, u32[]{:S(2)}, u32[]{:S(2)}) collective-permute-start(bf16[32,1,8,128]{3,0,2,1:T(8,128)(2,1)} %get-tuple-element.377), channel_id=1, source_target_pairs={{0,4},{4,8},{8,12},{12,16},{16,20},{20,24},{24,28},{28,32},{32,36}... | collective-permute-start | bytes 196616 | tf_op jit(solution)/shard_map/ppermute | solution.py:16
  452.3 83.0 %collective-permute-start.17 = (bf16[32,1,8,128]{3,0,2,1:T(8,128)(2,1)}, bf16[32,1,8,128]{3,0,2,1:T(8,128)(2,1)S(1)}, u32[]{:S(2)}, u32[]{:S(2)}) collective-permute-start(bf16[32,1,8,128]{3,0,2,1:T(8,128)(2,1)} %get-tuple-element.378), channel_id=1, source_target_pairs={{4,0},{8,4},{12,8},{16,12},{20,16},{24,20},{28,24},{32,28},{36,32}... | collective-permute-start | bytes 196616 | tf_op jit(solution)/shard_map/ppermute | solution.py:18
  535.4 6.6 %collective-permute-start.18 = (bf16[32,6,1,128]{3,0,2,1:T(8,128)(2,1)S(1)}, bf16[32,6,1,128]{3,0,2,1:T(8,128)(2,1)S(1)}, u32[]{:S(2)}, u32[]{:S(2)}) collective-permute-start(bf16[32,6,1,128]{3,0,2,1:T(8,128)(2,1)S(1)} %get-tuple-element.363), channel_id=1, source_target_pairs={{0,1},{1,2},{2,3},{4,5},{5,6},{6,7},{8,9},{9,10},{10,11},{12,13},{... | collective-permute-start | bytes 147464 | tf_op jit(solution)/shard_map/ppermute | solution.py:16
  539.2 6.9 %collective-permute-start.19 = (bf16[32,6,1,128]{3,0,2,1:T(8,128)(2,1)S(1)}, bf16[32,6,1,128]{3,0,2,1:T(8,128)(2,1)S(1)}, u32[]{:S(2)}, u32[]{:S(2)}) collective-permute-start(bf16[32,6,1,128]{3,0,2,1:T(8,128)(2,1)S(1)} %get-tuple-element.364), channel_id=1, source_target_pairs={{1,0},{2,1},{3,2},{5,4},{6,5},{7,6},{9,8},{10,9},{11,10},{13,12},{... | collective-permute-start | bytes 147464 | tf_op jit(solution)/shard_map/ppermute | solution.py:18
  549.8 7.3 %copy-start.4 = (bf16[8,128,128]{2,1,0:T(8,128)(2,1)S(1)}, bf16[8,128,128]{2,1,0:T(8,128)(2,1)}, u32[]{:S(2)}) copy-start(bf16[8,128,128]{2,1,0:T(8,128)(2,1)} %param.15) | copy-start | bytes 786436
  557.1 54.1 %copy-start.1 = (bf16[16,4,128]{2,1,0:T(4,128)(2,1)S(1)}, bf16[16,4,128]{2,1,0:T(4,128)(2,1)}, u32[]{:S(2)}) copy-start(bf16[16,4,128]{2,1,0:T(4,128)(2,1)} %param.14) | copy-start | bytes 49156
  (40 other events, 154.0 us)
Sparse Core Ops, SparseCore 0:
  38.3 34.8 reduce-scatter.1
  157.4 252.5 all-reduce.14
where the time goes:
time: 628 us; the launch traced here: 618 us
  waiting for transfers between devices  275 us (44%)
  blocking collectives  86.5 us (14%)
  matrix products  72.4 us (12%)
  starting transfers between devices  70.2 us (11%)
  other arithmetic  51.7 us (8%)
  local copies, waits for them, and re-layouts  44 us (7%)
  between operations  16.3 us (3%)
    psum x1, waiting for transfers between devices, shards(): summed = lax.psum((d_first, d_middle, d_last), ('slab', 'view'))  240 us
    psum x1, blocking collectives, shards(): summed = lax.psum((d_first, d_middle, d_last), ('slab', 'view'))  80.9 us
    ppermute x12, starting transfers between devices, with_halo(): lax.ppermute(tail, axis, [(i, (i + 1) % count) for i in range(ends)])  50 us
    dot_general x135, matrix products, convolve(): jnp.einsum('oc,czyx->ozyx', kernel[za, yb, xc], parts[xc][:, za:za + dept...  40 us
    scatter-add x16, other arithmetic, fold_add_view(): jax.ops.segment_sum(jnp.take(proj, source.reshape(-1), axis=0), target.re...  38.8 us
    dot_general x81, matrix products, kernel_grad(): jnp.einsum('ozyx,czyx->oc', dout, parts[xc][:, za:za + depth, yb:yb + row...  31.9 us
    ppermute x12, waiting for transfers between devices, with_halo(): lax.ppermute(head, axis, [((i + 1) % count, i) for i in range(ends)])  30.4 us
    ppermute x12, starting transfers between devices, with_halo(): lax.ppermute(head, axis, [((i + 1) % count, i) for i in range(ends)])  20.1 us
  transfers between devices with their start and end apart: 26, of which 10 were waited for; matrix products, arithmetic and copies ran while one was open for 4% of the time, Pallas kernels for 0%

commit v1 on v0

--- a/solution.py
+++ b/solution.py
@@ -153,7 +153,8 @@
     d_dual = lax.fori_loop(0, views_here, fold_add_view, start_grad).reshape(
         views_here, det_tiles, bins
     )
-    summed = lax.psum((d_first, d_middle, d_last), ("slab", "view"))
+    half = lax.psum((d_first, d_middle, d_last), "view")
+    summed = lax.psum(half, "slab")
     scale = 1.0 / math.sqrt(depth * lax.axis_size("slab") * full_rows * width)
     return (d_primal, d_dual, summed[0] * scale, summed[1] * scale, summed[2] * scale)
 

time: 628 us -> 890 us (1.42)
  blocking collectives: 86.5 us -> 321 us
  starting transfers between devices: 70.2 us -> 122 us
  waiting for transfers between devices: 275 us -> 231 us
  matrix products: 72.4 us -> 87.1 us
    psum x1 -> x2, blocking collectives: 80.9 us -> 273 us  [the longest x1 256 us: shards(): summed = lax.psum(half, 'slab')]
    ppermute x12, starting transfers between devices: 50 us -> 101 us  [with_halo(): lax.ppermute(tail, axis, [(i, (i + 1) % count) for i in range(ends)])]
    all_gather x1, blocking collectives: 5.59 us -> 48.3 us  [shards(): piece = lax.all_gather(strip_grad, 'view', axis=1, tiled=True)]
    psum x1 -> x2, waiting for transfers between devices: 240 us -> 200 us  [the longest x1 172 us: shards(): summed = lax.psum(half, 'slab')]
    dot_general x81, matrix products: 31.9 us -> 48 us  [kernel_grad(): jnp.einsum('ozyx,czyx->oc', dout, parts[xc][:, za:za + depth, yb:yb + row...]
  transfers between devices with their start and end apart: 26 -> 27, of which waited for: 10 -> 10; matrix products, arithmetic and copies ran while one was open for 4% -> 7% of each run, Pallas kernels for 0% -> 0%
where the time goes in v1:
time: 890 us; the launch traced here: 880 us
  blocking collectives  321 us (36%)
  waiting for transfers between devices  231 us (26%)
  starting transfers between devices  122 us (14%)
  matrix products  87.1 us (10%)
  other arithmetic  57.1 us (6%)
  local copies, waits for them, and re-layouts  44 us (5%)
  between operations  16.1 us (2%)
    psum x1, blocking collectives, shards(): summed = lax.psum(half, 'slab')  256 us
    psum x1, waiting for transfers between devices, shards(): summed = lax.psum(half, 'slab')  172 us
    ppermute x12, starting transfers between devices, with_halo(): lax.ppermute(tail, axis, [(i, (i + 1) % count) for i in range(ends)])  101 us
    all_gather x1, blocking collectives, shards(): piece = lax.all_gather(strip_grad, 'view', axis=1, tiled=True)  48.3 us
    dot_general x81, matrix products, kernel_grad(): jnp.einsum('ozyx,czyx->oc', dout, parts[xc][:, za:za + depth, yb:yb + row...  48 us
    scatter-add x16, other arithmetic, fold_add_view(): jax.ops.segment_sum(jnp.take(proj, source.reshape(-1), axis=0), target.re...  38.8 us
    dot_general x135, matrix products, convolve(): jnp.einsum('oc,czyx->ozyx', kernel[za, yb, xc], parts[xc][:, za:za + dept...  38.6 us
    psum x1, waiting for transfers between devices, shards(): half = lax.psum((d_first, d_middle, d_last), 'view')  28.1 us
  transfers between devices with their start and end apart: 27, of which 10 were waited for; matrix products, arithmetic and copies ran while one was open for 7% of the time, Pallas kernels for 0%

profile of v1, /device:TPU:1, one launch (start us, length us, event | category | flops | bytes accessed | tf_op | source)
XLA Modules:
  0.0 880.0 jit_solution(795080830807781845)
XLA Ops:
  7.3 3.5 copy.388
  10.8 2.7 copy.389
  15.8 21.8 %while.30 = (s32[]{:T(128)}, f32[4,32,1,128]{3,2,1,0:T(1,128)S(1)}, s32[16,4,32,1,2]{4,2,1,3,0:T(8,128)S(1)}, s32[16,4,32,1,2]{4,2,1,3,0:T(8,128)S(1)}, f32[512,...) while((s32[]{:T(128)}, f32[4,32,1,128]{3,2,1,0:T(1,128)S(1)}, ...), condition=%wide.region_2.3_spmd.clone, body=%wide.region_0.2_spmd.clone.sunk | while | flops 86788 | bytes 669307 | solution.py:104
  38.3 4.4 collective-permute-start
  44.9 2.4 collective-permute-done.1
  47.3 6.5 collective-permute-start.2
  53.8 1.9 collective-permute-start.3
  55.7 4.6 collective-permute-done.3
  68.0 5.2 reduce-scatter.2.cloned.1.call-done
  73.9 3.2 collective-permute-start.4
  78.7 2.8 collective-permute-done.5
  81.6 4.7 collective-permute-start.6
  88.3 4.6 collective-permute-done.7
  106.4 3.2 collective-permute-start.8
  112.4 2.8 collective-permute-done.9
  115.2 3.1 collective-permute-start.10
  120.3 4.9 collective-permute-done.11
  154.0 4.8 collective-permute-start.20
  164.2 4.3 collective-permute-start.12
  170.4 2.4 collective-permute-start.22
  172.9 2.5 collective-permute-start.23
  176.1 4.6 collective-permute-start.14
  180.6 2.1 collective-permute-start.15
  183.6 28.1 %all-reduce.17.cloned.1.call-done = f32[3,3,3,32,32]{4,3,2,1,0:T(8,128)} async-done(((f32[3,3,3,32,32]{4,3,2,1,0:T(8,128)}), f32[3,3,3,32,32]{4,3,2,1,0:T(8,128)}) %all-reduce.17.cloned.1.call-update) | async-done | bytes 110608 | tf_op jit(solution)/shard_map/psum | solution.py:156
  250.6 16.2 %all-reduce.13 = (f32[3,3,3,32,6]{3,4,2,1,0:T(8,128)S(1)}, f32[3,3,3,5,32]{4,2,3,1,0:T(4,128)S(1)}) all-reduce(f32[3,3,3,32,6]{3,4,2,1,0:T(8,128)} %bitcast.559, f32[3,3,3,5,32]{4,2,3,1,0:T(4,128)S(1)} %copy.582), channel_id=1, replica_groups=mesh['slab'=64,'view'=4] {'view'}, use_global_device_ids=true, to_apply=%region_7.8 | all-reduce | flops 9504 | bytes 76032 | tf_op jit(solution)/shard_map/psum | solution.py:156
  266.9 256.4 %all-reduce.12 = (f32[3,3,3,32,6]{3,4,2,1,0:T(8,128)S(1)}, f32[3,3,3,5,32]{4,2,3,1,0:T(4,128)S(1)}) all-reduce(f32[3,3,3,32,6]{3,4,2,1,0:T(8,128)S(1)} %get-tuple-element.301, f32[3,3,3,5,32]{4,2,3,1,0:T(4,128)S(1)} %get-tuple-element.302), channel_id=1, replica_groups=mesh['slab'=64,'view'=4] {'slab'}, use_global_device_ids=true, to_apply=%region_8.9 | all-reduce | flops 9504 | bytes 76032 | tf_op jit(solution)/shard_map/psum | solution.py:157
  527.3 3.0 collective-permute-done.17
  530.3 58.9 %collective-permute-start.18 = (bf16[32,6,1,128]{3,0,2,1:T(8,128)(2,1)S(1)}, bf16[32,6,1,128]{3,0,2,1:T(8,128)(2,1)S(1)}, u32[]{:S(2)}, u32[]{:S(2)}) collective-permute-start(bf16[32,6,1,128]{3,0,2,1:T(8,128)(2,1)S(1)} %get-tuple-element.365), channel_id=1, source_target_pairs={{0,1},{1,2},{2,3},{4,5},{5,6},{6,7},{8,9},{9,10},{10,11},{12,13},{... | collective-permute-start | bytes 147464 | tf_op jit(solution)/shard_map/ppermute | solution.py:16
  589.2 2.1 collective-permute-start.19
  591.4 172.2 %all-reduce.19.cloned.1.call-done = f32[3,3,3,32,32]{4,3,2,1,0:T(8,128)} async-done(((f32[3,3,3,32,32]{4,3,2,1,0:T(8,128)}), f32[3,3,3,32,32]{4,3,2,1,0:T(8,128)}) %all-reduce.19.cloned.1.call-update) | async-done | bytes 110608 | tf_op jit(solution)/shard_map/psum | solution.py:157
  770.8 48.3 %all-gather = bf16[1,4,32,128]{3,0,2,1:T(2,128)(2,1)S(1)} all-gather(bf16[1,4,8,128]{3,0,2,1:T(2,128)(2,1)S(1)} %slice.2106), channel_id=2, replica_groups=mesh['slab'=64,'view'=4] {'view'}, dimensions={2}, use_global_device_ids=true | all-gather | bytes 40960 | tf_op jit(solution)/shard_map/all_gather | solution.py:135
  819.5 53.1 %while.29 = (s32[]{:T(128)}, f32[64,128]{1,0:T(8,128)S(1)}, s32[16,4,32,1,2]{4,2,1,3,0:T(8,128)S(1)}, s32[16,4,32,1,2]{4,2,1,3,0:T(8,128)S(1)}, f32[1024,128]{1,...) while((s32[]{:T(128)}, f32[64,128]{1,0:T(8,128)S(1)}, ...), condition=%wide.region_6.7_spmd.clone.clone, body=%wide.region_4.6_spmd.clone.clone.sunk | while | flops 70019 | bytes 588653 | solution.py:153
  820.4 2.4 scatter_custom_fusion.6
  823.7 2.4 scatter_custom_fusion.6
  827.0 2.4 scatter_custom_fusion.6
  830.3 2.4 scatter_custom_fusion.6
  833.7 2.4 scatter_custom_fusion.6
  837.0 2.4 scatter_custom_fusion.6
  840.3 2.4 scatter_custom_fusion.6
  843.6 2.4 scatter_custom_fusion.6
  846.9 2.4 scatter_custom_fusion.6
  850.2 2.4 scatter_custom_fusion.6
  853.6 2.4 scatter_custom_fusion.6
  856.9 2.4 scatter_custom_fusion.6
  860.2 2.4 scatter_custom_fusion.6
  863.5 2.4 scatter_custom_fusion.6
  866.8 2.4 scatter_custom_fusion.6
  870.1 2.4 scatter_custom_fusion.6
  (735 shorter events, 156.8 us)
Async XLA Ops:
  7.2 66.0 %reduce-scatter.2.cloned.1.call-start = ((), (), s32[]{:S(2)}) async-start(), calls=%async_computation.1 | async-start | bytes 81920 | tf_op jit(solution)/shard_map/reduce_scatter | solution.py:107
  15.7 22.5 %copy-start.6 = (f32[5,4,8,128]{3,2,1,0:T(8,128)S(1)}, f32[5,4,8,128]{3,2,1,0:T(8,128)}, u32[]{:S(2)}) copy-start(f32[5,4,8,128]{3,2,1,0:T(8,128)} %param.21) | copy-start | bytes 245764
  15.7 28.2 %copy-start.60 = (bf16[3,3,3,5,32]{4,2,3,1,0:T(4,128)(2,1)S(1)}, bf16[3,3,3,5,32]{4,2,3,1,0:T(4,128)(2,1)}, u32[]{:S(2)}) copy-start(bf16[3,3,3,5,32]{4,2,3,1,0:T(4,128)(2,1)} %param.20) | copy-start | bytes 25924
  15.8 28.3 %copy-start.5 = (bf16[3,3,3,32,32]{4,3,2,1,0:T(8,128)(2,1)S(1)}, bf16[3,3,3,32,32]{4,3,2,1,0:T(8,128)(2,1)}, u32[]{:S(2)}) copy-start(bf16[3,3,3,32,32]{4,3,2,1,0:T(8,128)(2,1)} %param.19) | copy-start | bytes 165892
  15.8 28.5 %copy-start.51 = (bf16[3,3,3,32,6]{3,4,2,1,0:T(8,128)(2,1)S(1)}, bf16[3,3,3,32,6]{3,4,2,1,0:T(8,128)(2,1)}, u32[]{:S(2)}) copy-start(bf16[3,3,3,32,6]{3,4,2,1,0:T(8,128)(2,1)} %param.18) | copy-start | bytes 31108
  15.8 29.1 %copy-start.55 = (f32[5,4,8,128]{3,2,1,0:T(8,128)S(1)}, f32[5,4,8,128]{3,2,1,0:T(8,128)}, u32[]{:S(2)}) copy-start(f32[5,4,8,128]{3,2,1,0:T(8,128)} %param.13) | copy-start | bytes 245764
  38.2 173.4 %all-reduce.17.cloned.1.call-start = ((), (), s32[]{:S(2)}) async-start(), calls=%async_computation.2 | async-start | bytes 884736 | tf_op jit(solution)/shard_map/psum | solution.py:156
  38.3 6.6 collective-permute-start
  42.7 4.6 collective-permute-start.1
  44.0 34.4 %copy-start.53 = (bf16[3,3,3,32,5]{3,4,2,1,0:T(8,128)(2,1)}, bf16[3,3,3,32,5]{3,4,2,1,0:T(8,128)(2,1)S(1)}, u32[]{:S(2)}) copy-start(bf16[3,3,3,32,5]{3,4,2,1,0:T(8,128)(2,1)S(1)} %reverse_bitcast_fusion.2) | copy-start | bytes 25924
  47.3 8.4 collective-permute-start.2
  53.8 6.6 collective-permute-start.3
  73.9 4.8 collective-permute-start.4
  77.1 4.4 collective-permute-start.5
  78.4 21.2 %copy-start.52 = (bf16[3,3,3,32,6]{3,4,2,1,0:T(8,128)(2,1)S(1)}, bf16[3,3,3,32,6]{3,4,2,1,0:T(8,128)(2,1)}, u32[]{:S(2)}) copy-start(bf16[3,3,3,32,6]{3,4,2,1,0:T(8,128)(2,1)} %param.18) | copy-start | bytes 31108
  81.6 6.7 collective-permute-start.6
  86.3 6.6 collective-permute-start.7
  88.3 12.0 %copy-start.17 = (bf16[6,4,8,128]{3,2,1,0:T(8,128)(2,1)}, bf16[6,4,8,128]{3,2,1,0:T(8,128)(2,1)S(1)}, u32[]{:S(2)}) copy-start(bf16[6,4,8,128]{3,2,1,0:T(8,128)(2,1)S(1)} %get-tuple-element.448) | copy-start | bytes 147460
  106.4 5.9 collective-permute-start.8
  109.6 5.6 collective-permute-start.9
  115.2 5.1 collective-permute-start.10
  118.3 6.9 collective-permute-start.11
  154.0 15.7 %collective-permute-start.20 = (bf16[32,1,8,128]{3,0,2,1:T(8,128)(2,1)}, bf16[32,1,8,128]{3,0,2,1:T(8,128)(2,1)S(1)}, u32[]{:S(2)}, u32[]{:S(2)}) collective-permute-start(bf16[32,1,8,128]{3,0,2,1:T(8,128)(2,1)} %get-tuple-element.377), channel_id=1, source_target_pairs={{0,4},{4,8},{8,12},{12,16},{16,20},{20,24},{24,28},{28,32},{32,36}... | collective-permute-start | bytes 196616 | tf_op jit(solution)/shard_map/ppermute | solution.py:16
  158.9 10.9 %collective-permute-start.21 = (bf16[32,1,8,128]{3,0,2,1:T(8,128)(2,1)}, bf16[32,1,8,128]{3,0,2,1:T(8,128)(2,1)S(1)}, u32[]{:S(2)}, u32[]{:S(2)}) collective-permute-start(bf16[32,1,8,128]{3,0,2,1:T(8,128)(2,1)} %get-tuple-element.378), channel_id=1, source_target_pairs={{4,0},{8,4},{12,8},{16,12},{20,16},{24,20},{28,24},{32,28},{36,32}... | collective-permute-start | bytes 196616 | tf_op jit(solution)/shard_map/ppermute | solution.py:18
  164.1 599.5 %all-reduce.19.cloned.1.call-start = ((), (), s32[]{:S(2)}) async-start(), calls=%async_computation.3 | async-start | bytes 884736 | tf_op jit(solution)/shard_map/psum | solution.py:157
  164.2 11.2 %collective-permute-start.12 = (bf16[32,1,8,128]{3,0,2,1:T(8,128)(2,1)}, bf16[32,1,8,128]{3,0,2,1:T(8,128)(2,1)S(1)}, u32[]{:S(2)}, u32[]{:S(2)}) collective-permute-start(bf16[32,1,8,128]{3,0,2,1:T(8,128)(2,1)} %get-tuple-element.381), channel_id=1, source_target_pairs={{0,4},{4,8},{8,12},{12,16},{16,20},{20,24},{24,28},{28,32},{32,36}... | collective-permute-start | bytes 196616 | tf_op jit(solution)/shard_map/ppermute | solution.py:16
  168.5 6.9 collective-permute-start.13
  170.4 51.3 %collective-permute-start.22 = (bf16[32,6,1,128]{3,0,2,1:T(8,128)(2,1)}, bf16[32,6,1,128]{3,0,2,1:T(8,128)(2,1)}, u32[]{:S(2)}, u32[]{:S(2)}) collective-permute-start(bf16[32,6,1,128]{3,0,2,1:T(8,128)(2,1)} %get-tuple-element.363), channel_id=1, source_target_pairs={{0,1},{1,2},{2,3},{4,5},{5,6},{6,7},{8,9},{9,10},{10,11},{12,13},{... | collective-permute-start | bytes 147464 | tf_op jit(solution)/shard_map/ppermute | solution.py:16
  172.9 48.8 %collective-permute-start.23 = (bf16[32,6,1,128]{3,0,2,1:T(8,128)(2,1)}, bf16[32,6,1,128]{3,0,2,1:T(8,128)(2,1)}, u32[]{:S(2)}, u32[]{:S(2)}) collective-permute-start(bf16[32,6,1,128]{3,0,2,1:T(8,128)(2,1)} %get-tuple-element.364), channel_id=1, source_target_pairs={{1,0},{2,1},{3,2},{5,4},{6,5},{7,6},{9,8},{10,9},{11,10},{13,12},{... | collective-permute-start | bytes 147464 | tf_op jit(solution)/shard_map/ppermute | solution.py:18
  176.1 35.6 %collective-permute-start.14 = (bf16[32,6,1,128]{3,0,2,1:T(8,128)(2,1)}, bf16[32,6,1,128]{3,0,2,1:T(8,128)(2,1)}, u32[]{:S(2)}, u32[]{:S(2)}) collective-permute-start(bf16[32,6,1,128]{3,0,2,1:T(8,128)(2,1)} %get-tuple-element.369), channel_id=1, source_target_pairs={{0,1},{1,2},{2,3},{4,5},{5,6},{6,7},{8,9},{9,10},{10,11},{12,13},{... | collective-permute-start | bytes 147464 | tf_op jit(solution)/shard_map/ppermute | solution.py:16
  180.6 31.0 %collective-permute-start.15 = (bf16[32,6,1,128]{3,0,2,1:T(8,128)(2,1)}, bf16[32,6,1,128]{3,0,2,1:T(8,128)(2,1)}, u32[]{:S(2)}, u32[]{:S(2)}) collective-permute-start(bf16[32,6,1,128]{3,0,2,1:T(8,128)(2,1)} %get-tuple-element.370), channel_id=1, source_target_pairs={{1,0},{2,1},{3,2},{5,4},{6,5},{7,6},{9,8},{10,9},{11,10},{13,12},{... | collective-permute-start | bytes 147464 | tf_op jit(solution)/shard_map/ppermute | solution.py:18
  228.9 11.6 %copy-start.28 = (bf16[6,4,8,128]{3,2,1,0:T(8,128)(2,1)S(1)}, bf16[6,4,8,128]{3,2,1,0:T(8,128)(2,1)}, u32[]{:S(2)}) copy-start(bf16[6,4,8,128]{3,2,1,0:T(8,128)(2,1)} %copy-done.27) | copy-start | bytes 147460
  229.1 12.2 %copy-start.8 = (bf16[6,4,8,128]{3,2,1,0:T(8,128)(2,1)S(1)}, bf16[6,4,8,128]{3,2,1,0:T(8,128)(2,1)}, u32[]{:S(2)}) copy-start(bf16[6,4,8,128]{3,2,1,0:T(8,128)(2,1)} %copy-done.7) | copy-start | bytes 147460
  229.3 12.8 %copy-start.34 = (bf16[6,4,8,128]{3,2,1,0:T(8,128)(2,1)S(1)}, bf16[6,4,8,128]{3,2,1,0:T(8,128)(2,1)}, u32[]{:S(2)}) copy-start(bf16[6,4,8,128]{3,2,1,0:T(8,128)(2,1)} %copy-done.33) | copy-start | bytes 147460
  229.5 13.3 %copy-start.24 = (bf16[6,4,8,128]{3,2,1,0:T(8,128)(2,1)S(1)}, bf16[6,4,8,128]{3,2,1,0:T(8,128)(2,1)}, u32[]{:S(2)}) copy-start(bf16[6,4,8,128]{3,2,1,0:T(8,128)(2,1)} %copy-done.23) | copy-start | bytes 147460
  229.8 14.5 %copy-start.12 = (bf16[6,4,8,128]{3,2,1,0:T(8,128)(2,1)S(1)}, bf16[6,4,8,128]{3,2,1,0:T(8,128)(2,1)}, u32[]{:S(2)}) copy-start(bf16[6,4,8,128]{3,2,1,0:T(8,128)(2,1)} %copy-done.11) | copy-start | bytes 147460
  230.0 15.1 %copy-start.20 = (bf16[6,4,8,128]{3,2,1,0:T(8,128)(2,1)S(1)}, bf16[6,4,8,128]{3,2,1,0:T(8,128)(2,1)}, u32[]{:S(2)}) copy-start(bf16[6,4,8,128]{3,2,1,0:T(8,128)(2,1)} %copy-done.19) | copy-start | bytes 147460
  231.1 16.4 %copy-start.10 = (bf16[6,4,8,128]{3,2,1,0:T(8,128)(2,1)S(1)}, bf16[6,4,8,128]{3,2,1,0:T(8,128)(2,1)}, u32[]{:S(2)}) copy-start(bf16[6,4,8,128]{3,2,1,0:T(8,128)(2,1)} %copy-done.9) | copy-start | bytes 147460
  232.6 16.4 %copy-start.14 = (bf16[6,4,8,128]{3,2,1,0:T(8,128)(2,1)S(1)}, bf16[6,4,8,128]{3,2,1,0:T(8,128)(2,1)}, u32[]{:S(2)}) copy-start(bf16[6,4,8,128]{3,2,1,0:T(8,128)(2,1)} %copy-done.13) | copy-start | bytes 147460
  233.4 16.4 %copy-start.59 = (bf16[6,4,8,128]{3,2,1,0:T(8,128)(2,1)S(1)}, bf16[6,4,8,128]{3,2,1,0:T(8,128)(2,1)}, u32[]{:S(2)}) copy-start(bf16[6,4,8,128]{3,2,1,0:T(8,128)(2,1)} %copy-done.58) | copy-start | bytes 147460
  235.8 289.4 %copy-start.57 = (bf16[32,1,8,128]{3,0,2,1:T(8,128)(2,1)S(1)}, bf16[32,1,8,128]{3,0,2,1:T(8,128)(2,1)}, u32[]{:S(2)}) copy-start(bf16[32,1,8,128]{3,0,2,1:T(8,128)(2,1)} %get-tuple-element.380) | copy-start | bytes 196612
  235.8 290.7 %copy-start.54 = (bf16[3,3,3,6,32]{4,3,2,1,0:T(8,128)(2,1)S(1)}, bf16[3,3,3,6,32]{4,3,2,1,0:T(8,128)(2,1)}, u32[]{:S(2)}) copy-start(bf16[3,3,3,6,32]{4,3,2,1,0:T(8,128)(2,1)} %reverse_bitcast_fusion.1) | copy-start | bytes 31108
  523.9 3.4 collective-permute-start.16
  525.2 5.1 collective-permute-start.17
  530.3 235.1 %collective-permute-start.18 = (bf16[32,6,1,128]{3,0,2,1:T(8,128)(2,1)S(1)}, bf16[32,6,1,128]{3,0,2,1:T(8,128)(2,1)S(1)}, u32[]{:S(2)}, u32[]{:S(2)}) collective-permute-start(bf16[32,6,1,128]{3,0,2,1:T(8,128)(2,1)S(1)} %get-tuple-element.365), channel_id=1, source_target_pairs={{0,1},{1,2},{2,3},{4,5},{5,6},{6,7},{8,9},{9,10},{10,11},{12,13},{... | collective-permute-start | bytes 147464 | tf_op jit(solution)/shard_map/ppermute | solution.py:16
  589.2 176.2 %collective-permute-start.19 = (bf16[32,6,1,128]{3,0,2,1:T(8,128)(2,1)S(1)}, bf16[32,6,1,128]{3,0,2,1:T(8,128)(2,1)S(1)}, u32[]{:S(2)}, u32[]{:S(2)}) collective-permute-start(bf16[32,6,1,128]{3,0,2,1:T(8,128)(2,1)S(1)} %get-tuple-element.366), channel_id=1, source_target_pairs={{1,0},{2,1},{3,2},{5,4},{6,5},{7,6},{9,8},{10,9},{11,10},{13,12},{... | collective-permute-start | bytes 147464 | tf_op jit(solution)/shard_map/ppermute | solution.py:18
  769.1 50.0 %copy-start.4 = (bf16[8,128,128]{2,1,0:T(8,128)(2,1)S(1)}, bf16[8,128,128]{2,1,0:T(8,128)(2,1)}, u32[]{:S(2)}) copy-start(bf16[8,128,128]{2,1,0:T(8,128)(2,1)} %param.15) | copy-start | bytes 786436
  819.2 54.1 %copy-start.1 = (bf16[16,4,128]{2,1,0:T(4,128)(2,1)S(1)}, bf16[16,4,128]{2,1,0:T(4,128)(2,1)}, u32[]{:S(2)}) copy-start(bf16[16,4,128]{2,1,0:T(4,128)(2,1)} %param.14) | copy-start | bytes 49156
  (43 other events, 259.4 us)
Sparse Core Ops, SparseCore 0:
  38.3 34.8 reduce-scatter.1
  164.3 47.3 all-reduce.16
  214.3 549.3 all-reduce.18
